TPU v7x, 32 devices: a whole 2x2x4 slice. The times are simulated.
32 devices in a mesh: pair: 8 (over z, core), cd: 4 (over y, x).
Axes of the slice: x: 2, y: 2, z: 4, core: 2. Of those that a mesh axis runs over, the one named last changes fastest.
Arguments:
- amplitudes: float32 [2048, 4096], P('pair', 'cd'), may hold values from -6 to 6
- integrals: float32 [4096, 256], P(('cd', 'pair')), may hold values from -0.09375 to 0.09375
- keep_tiles: int32 [32, 2], replicated, may hold values from 0 to 1, as said below
Outputs:
- ladder: float32 [2048, 256], P(('pair', 'cd'))
Inputs may be any that keep to these rules, and one draw needn't show every extreme that they name: `keep_tiles`: each entry is 0 (tile screened out) or 1 (tile kept); each tile row keeps at most one tile, and some tile row keeps one.
All inputs are finite; a program needn't handle non-finite values.
Results may differ from a plain program's by a relative error of at most 0.000071.
Values sent between devices are 32-bit elements; how exact they have to be, the bound alone decides.
A program may use at most 64 MiB of HBM per device.

v0:
```python
import jax
import jax.numpy as jnp
from jax import lax
from jax.sharding import PartitionSpec as P

TILE = 128


def pack_kept(integrals, keep_tiles):
    blocks = integrals.shape[1] // TILE
    row_block = lax.axis_index("cd") * lax.axis_size("pair") + lax.axis_index("pair")
    flags = lax.dynamic_slice_in_dim(keep_tiles, row_block, 1, 0)[0].astype(jnp.float32)
    tiles = integrals.reshape(integrals.shape[0], blocks, TILE)
    return jnp.sum(tiles * flags[None, :, None], axis=1)


def local(amplitudes, integrals, keep_tiles):
    group_first = lax.axis_index("cd") * amplitudes.shape[1]
    empty = jnp.zeros((amplitudes.shape[0], integrals.shape[1]), jnp.float32)
    packed = pack_kept(integrals, keep_tiles)
    piece = lax.all_gather(packed, "pair", axis=0, tiled=True)
    count = piece.shape[0] // TILE
    flags = lax.dynamic_slice_in_dim(keep_tiles, group_first // TILE, count, 0).astype(jnp.float32)
    columns = amplitudes
    columns = columns.reshape(columns.shape[0], count, TILE)
    tiles = piece.reshape(count, TILE, TILE)
    products = jnp.einsum(
        "pnt,ntu->npu",
        columns,
        tiles,
        precision=lax.Precision.HIGHEST,
        preferred_element_type=jnp.float32,
    )
    placed = jnp.einsum(
        "npu,nm->pmu",
        products,
        flags,
        precision=lax.Precision.HIGHEST,
        preferred_element_type=jnp.float32,
    )
    partial_sum = placed.reshape(empty.shape)
    return lax.psum_scatter(partial_sum, "cd", scatter_dimension=0, tiled=True)


def solution(mesh):
    placed = (P("pair", "cd"), P(("cd", "pair"), None), P())
    return jax.shard_map(
        local, mesh=mesh, in_specs=placed, out_specs=P(("pair", "cd"), None), check_vma=False
    )
```

profile of v0, /device:TPU:0, one launch (start us, length us, event | category | flops | bytes accessed | tf_op | source)
XLA Modules:
  0.0 61.9 jit_solution(18389395214170806950)
XLA Ops:
  6.5 0.0 copy-start
  6.5 0.0 reduce-scatter.2.cloned.1.call-start
  6.5 1.1 %reshape.18 = f32[128,2,128]{2,1,0:T(2,128)S(1)} reshape(f32[128,256]{1,0:T(8,128)} %param.4) | data formatting | bytes 262144 | tf_op jit(solution)/shard_map/reshape | solution.py:13
  7.6 0.9 %convert_reduce_fusion = f32[2]{0:T(128)S(1)} fusion(s32[32,2]{0,1:T(2,128)} %param.5, s32[]{:T(128)S(6)} %select_n.13), kind=kLoop, calls=%fused_computation.5 | loop fusion | flops 2 | bytes 20 | tf_op jit(solution)/shard_map/convert_element_type | solution.py:12
  8.5 0.2 multiply_reduce_fusion
  8.7 16.5 %all_gather.3 = f32[1024,128]{1,0:T(8,128)S(1)} all-gather(f32[128,128]{1,0:T(8,128)S(1)} %multiply_reduce_fusion), channel_id=1, replica_groups=mesh['pair'=8,'cd'=4] {'pair'}, dimensions={0}, use_global_device_ids=true | all-gather | bytes 589824 | tf_op jit(solution)/shard_map/all_gather | solution.py:21
  25.2 0.0 copy-done
  25.2 0.3 copy.6
  25.5 1.0 %fusion.6 = f32[8,128,256]{2,1,0:T(8,128)S(1)} fusion(f32[8,128,128]{2,1,0:T(8,128)S(1)} %bitcast.16, f32[256,8,128]{0,2,1:T(8,128)S(1)} %bitcast.15), kind=kOutput, calls=%fused_computation.9 | convolution fusion | flops 402653184 | bytes 2621440 | tf_op jit(solution)/shard_map/pnt,ntu->npu/dot_general | solution.py:27
  26.6 0.4 copy.5
  27.0 0.0 copy-start.1
  27.0 0.7 %copy-done.1 = s32[32,2]{0,1:T(2,128)S(1)} copy-done((s32[32,2]{0,1:T(2,128)S(1)}, s32[32,2]{0,1:T(2,128)}, u32[]{:S(2)}) %copy-start.1) | copy-done | bytes 280
  27.7 1.0 %fusion = f32[2,256,128]{2,0,1:T(2,128)S(1)} fusion(f32[8,128,256]{1,0,2:T(8,128)S(1)} %copy.5, s32[32,2]{0,1:T(2,128)S(1)} %copy-done.1, s32[]{:T(128)S(6)} %select_n.12), kind=kOutput, calls=%fused_computation | convolution fusion | flops 6291472 | bytes 1310980 | tf_op jit(solution)/shard_map/npu,nm->pmu/dot_general | solution.py:34
  28.7 0.7 %copy.9 = f32[32,8,2,128]{3,1,2,0:T(8,128)} copy(f32[32,8,2,128]{3,2,1,0:T(2,128)S(1)} %bitcast.18) | data formatting | bytes 524288
  29.4 0.0 reduce-scatter.2.cloned.1.call-update
  29.5 25.5 %reduce-scatter.2.cloned.1.call-done = f32[64,256]{1,0:T(8,128)} async-done(((f32[256,256]{1,0:T(8,128)}), f32[64,256]{1,0:T(8,128)}) %reduce-scatter.2.cloned.1.call-update) | async-done | bytes 65552 | tf_op jit(solution)/shard_map/reduce_scatter | solution.py:42
Async XLA Ops:
  6.5 18.7 %copy-start = (f32[256,1024]{1,0:T(8,128)S(1)}, f32[256,1024]{1,0:T(8,128)}, u32[]{:S(2)}) copy-start(f32[256,1024]{1,0:T(8,128)} %param.3) | copy-start | bytes 3145732
  6.5 48.5 %reduce-scatter.2.cloned.1.call-start = ((), (), s32[]{:S(2)}) async-start(), calls=%async_computation.1 | async-start | bytes 327680 | tf_op jit(solution)/shard_map/reduce_scatter | solution.py:42
  27.0 0.7 %copy-start.1 = (s32[32,2]{0,1:T(2,128)S(1)}, s32[32,2]{0,1:T(2,128)}, u32[]{:S(2)}) copy-start(s32[32,2]{0,1:T(2,128)} %param.5) | copy-start | bytes 772
Sparse Core Ops, SparseCore 0:
  29.6 25.3 reduce-scatter.1
where the time goes:
time: 62 us; the launch traced here: 61.9 us
  waiting for transfers between devices  25.6 us (41%)
  blocking collectives  16.5 us (27%)
  between operations  13.4 us (22%)
  local copies, waits for them, and re-layouts  3.18 us (5%)
  matrix products  2.08 us (3%)
  other arithmetic  1.1 us (2%)
    reduce_scatter x1, waiting for transfers between devices, local(): return lax.psum_scatter(partial_sum, 'cd', scatter_dimension=0, tiled=True)  25.5 us
    all_gather x1, blocking collectives, local(): piece = lax.all_gather(packed, 'pair', axis=0, tiled=True)  16.5 us
    unnamed x5, local copies, waits for them, and re-layouts  1.38 us
  transfers between devices with their start and end apart: 1, of which 1 were waited for; matrix products, arithmetic and copies ran while one was open for 0% of the time, Pallas kernels for 0%

commit v1 on v0

v1 whole, which is shorter than its diff:
```python
import functools

import jax
import jax.numpy as jnp
from jax import lax
from jax.experimental import pallas as pl
from jax.experimental.pallas import tpu as pltpu
from jax.sharding import PartitionSpec as P

TILE = 128
CORES = 2
CHUNKS = 2
MESH = pl.DeviceIdType.MESH


def flip(i, bits):
    b = 1
    out = i
    while b <= bits:
        if bits & b:
            out = out + b - 2 * b * (lax.rem(lax.div(i, b), 2))
        b *= 2
    return out


def split(x):
    hi = x.astype(jnp.bfloat16)
    lo = (x - hi.astype(jnp.float32)).astype(jnp.bfloat16)
    return hi, lo


def dot3(a_hi, a_lo, b_hi, b_lo):
    d = functools.partial(jnp.dot, preferred_element_type=jnp.float32)
    return d(a_hi, b_hi) + (d(a_lo, b_hi) + d(a_hi, b_lo))


def kernel(pairs, cds, flags, v_hbm, a_hbm, out_ref, v, a, tiles, a_hi, a_lo, acc, land,
           load_sem, ssem, rsem, psend, precv, rs_send, rs_recv):
    nz = pairs // CORES
    me = lax.axis_index("pair")
    cd = lax.axis_index("cd")
    z = lax.div(me, CORES)
    core = lax.rem(me, CORES)
    partner = me + 1 - 2 * core
    blocks = v.shape[1] // TILE
    part = TILE // CHUNKS
    rows = out_ref.shape[0]

    load_v = pltpu.make_async_copy(v_hbm, v, load_sem.at[0])
    load_v.start()
    load_a = pltpu.make_async_copy(a_hbm, a, load_sem.at[1])
    load_a.start()

    has_next = (z + 1 < nz, z > 0)
    neighbour = (me + CORES, me - CORES)

    barrier = pltpu.get_barrier_semaphore()
    for d in range(2):
        @pl.when(has_next[d])
        def _():
            pl.semaphore_signal(barrier, inc=1, device_id={"pair": neighbour[d]}, device_id_type=MESH)
    pl.semaphore_signal(barrier, inc=1, device_id={"pair": partner}, device_id_type=MESH)
    for j in range(1, cds):
        pl.semaphore_signal(barrier, inc=1, device_id={"cd": flip(cd, j)}, device_id_type=MESH)

    load_v.wait()
    row_block = cd * pairs + me
    own = v[:, :TILE] * flags[row_block, 0].astype(jnp.float32)
    for m in range(1, blocks):
        own = own + v[:, m * TILE:(m + 1) * TILE] * flags[row_block, m].astype(jnp.float32)
    tiles[me] = own

    greeted = cds + jnp.minimum(z, 1) + jnp.minimum(nz - 1 - z, 1)
    pl.semaphore_wait(barrier, greeted)

    def stream(d, s, c, k):
        r = pl.ds(c * part, part)
        return pltpu.make_async_remote_copy(
            src_ref=tiles.at[k, r], dst_ref=tiles.at[k, r],
            send_sem=ssem.at[d, s, c], recv_sem=rsem.at[d, s, c],
            device_id={"pair": neighbour[d]}, device_id_type=MESH)

    def exchange(d, s, c, k):
        r = pl.ds(c * part, part)
        return pltpu.make_async_remote_copy(
            src_ref=tiles.at[k, r], dst_ref=tiles.at[k, r],
            send_sem=psend.at[d, s, c], recv_sem=precv.at[d, s, c],
            device_id={"pair": partner}, device_id_type=MESH)

    def origin(d, s):
        return z - s if d == 0 else z + s

    def valid(d, s):
        return z - s >= 0 if d == 0 else z + s < nz

    for c in range(CHUNKS):
        for d in range(2):
            @pl.when(has_next[d])
            def _():
                stream(d, 0, c, me).start()
    for c in range(CHUNKS):
        exchange(0, 0, c, me).start()

    load_a.wait()
    hi, lo = split(a[...])
    a_hi[...] = hi
    a_lo[...] = lo

    def compute(d, s):
        chip = origin(d, s)
        for c in range(CHUNKS):
            exchange(d, s, c, chip * CORES + 1 - core).wait_recv()
        halves = []
        for i in range(CORES):
            k = chip * CORES + i
            t = tiles[k]
            g = cd * pairs + k
            halves.append(jnp.concatenate(
                [t * flags[g, m].astype(jnp.float32) for m in range(blocks)], axis=1))
        b_hi, b_lo = split(jnp.concatenate(halves, axis=0))
        cols = pl.ds(pl.multiple_of(chip * (CORES * TILE), CORES * TILE), CORES * TILE)
        prod = dot3(a_hi[:, cols], a_lo[:, cols], b_hi, b_lo)
        if s == 0:
            acc[...] = prod
        else:
            acc[...] += prod

    for s in range(1, nz):
        for c in range(CHUNKS):
            for d in range(2):
                @pl.when(valid(d, s))
                def _():
                    k = origin(d, s) * CORES + core
                    stream(d, s - 1, c, k).wait_recv()
                    if s < nz - 1:
                        @pl.when(has_next[d])
                        def _():
                            stream(d, s, c, k).start()
                    exchange(d, s, c, k).start()
        if s == 1:
            compute(0, 0)
        else:
            for d in range(2):
                @pl.when(valid(d, s - 1))
                def _():
                    compute(d, s - 1)
    for d in range(2):
        @pl.when(valid(d, nz - 1))
        def _():
            compute(d, nz - 1)

    def scatter(j):
        q = flip(cd, j)
        return pltpu.make_async_remote_copy(
            src_ref=acc.at[pl.ds(pl.multiple_of(q * rows, rows), rows)], dst_ref=land.at[j - 1],
            send_sem=rs_send.at[j - 1], recv_sem=rs_recv.at[j - 1],
            device_id={"cd": q}, device_id_type=MESH)

    for j in range(cds - 1, 0, -1):
        scatter(j).start()

    for c in range(CHUNKS):
        exchange(0, 0, c, me).wait_send()
        for d in range(2):
            @pl.when(has_next[d])
            def _():
                stream(d, 0, c, me).wait_send()
    for s in range(1, nz):
        for d in range(2):
            @pl.when(valid(d, s))
            def _():
                k = origin(d, s) * CORES + core
                for c in range(CHUNKS):
                    exchange(d, s, c, k).wait_send()
                if s < nz - 1:
                    @pl.when(has_next[d])
                    def _():
                        for c in range(CHUNKS):
                            stream(d, s, c, k).wait_send()

    total = acc[pl.ds(pl.multiple_of(cd * rows, rows), rows)]
    for j in range(1, cds):
        scatter(j).wait_recv()
        total = total + land[j - 1]
    out_ref[...] = total
    for j in range(1, cds):
        scatter(j).wait_send()


def solution(mesh):
    pairs, cds = mesh.shape["pair"], mesh.shape["cd"]
    nz = pairs // CORES

    def local(amplitudes, integrals, keep_tiles):
        n, depth = amplitudes.shape
        ab = integrals.shape[1]
        rows = n // cds
        return pl.pallas_call(
            functools.partial(kernel, pairs, cds),
            out_shape=jax.ShapeDtypeStruct((rows, ab), jnp.float32),
            in_specs=[
                pl.BlockSpec(memory_space=pltpu.SMEM),
                pl.BlockSpec(memory_space=pl.ANY),
                pl.BlockSpec(memory_space=pl.ANY),
            ],
            out_specs=pl.BlockSpec(memory_space=pltpu.VMEM),
            scratch_shapes=[
                pltpu.VMEM(integrals.shape, jnp.float32),
                pltpu.VMEM((n, depth), jnp.float32),
                pltpu.VMEM((pairs, TILE, TILE), jnp.float32),
                pltpu.VMEM((n, depth), jnp.bfloat16),
                pltpu.VMEM((n, depth), jnp.bfloat16),
                pltpu.VMEM((n, ab), jnp.float32),
                pltpu.VMEM((cds - 1, rows, ab), jnp.float32),
                pltpu.SemaphoreType.DMA((2,)),
                pltpu.SemaphoreType.DMA((2, nz, CHUNKS)),
                pltpu.SemaphoreType.DMA((2, nz, CHUNKS)),
                pltpu.SemaphoreType.DMA((2, nz, CHUNKS)),
                pltpu.SemaphoreType.DMA((2, nz, CHUNKS)),
                pltpu.SemaphoreType.DMA((cds - 1,)),
                pltpu.SemaphoreType.DMA((cds - 1,)),
            ],
            compiler_params=pltpu.CompilerParams(collective_id=0, has_side_effects=True),
        )(keep_tiles, integrals, amplitudes)

    placed = (P("pair", "cd"), P(("cd", "pair"), None), P())
    return jax.shard_map(
        local, mesh=mesh, in_specs=placed, out_specs=P(("pair", "cd"), None), check_vma=False
    )
```

time: 62 us -> 25.3 us (0.41)
  waiting for transfers between devices: 25.6 us -> 0 us
  Pallas kernels: 0 us -> 22.2 us
  blocking collectives: 16.5 us -> 0 us
  between operations: 13.4 us -> 0.01 us
  matrix products: 2.08 us -> 0 us
  other arithmetic: 1.1 us -> 0 us
    reduce_scatter x1 -> x0, waiting for transfers between devices: 25.5 us -> none  [local(): return lax.psum_scatter(partial_sum, 'cd', scatter_dimension=0, tiled=True)]
    pallas_call x0 -> x1, Pallas kernels: none -> 22.2 us  [local(): pl.pallas_call(functools.partial(kernel, pairs, cds), out_shape=jax.Shape...]
    all_gather x1 -> x0, blocking collectives: 16.5 us -> none  [local(): piece = lax.all_gather(packed, 'pair', axis=0, tiled=True)]
    dot_general x2 -> x0, matrix products: 2.08 us -> none  [the longest x1 1.04 us: local(): jnp.einsum('npu,nm->pmu', products, flags, precision=lax.Precision.HIGHES...]
    unnamed x5 -> x2, local copies, waits for them, and re-layouts: 1.38 us -> 2.84 us
    reshape x2 -> x0, local copies, waits for them, and re-layouts: 1.39 us -> none  [the longest x1 1.06 us: pack_kept(): tiles = integrals.reshape(integrals.shape[0], blocks, TILE)]
    convert_element_type x1 -> x0, other arithmetic: 0.87 us -> none  [pack_kept(): lax.dynamic_slice_in_dim(keep_tiles, row_block, 1, 0)[0].astype(jnp.float32)]
  transfers between devices with their start and end apart: 1 -> 0, of which waited for: 1 -> 0; matrix products, arithmetic and copies ran while one was open for 0% -> 0% of each run, Pallas kernels for 0% -> 0%
where the time goes in v1:
time: 25.3 us; the launch traced here: 25 us
  Pallas kernels  22.2 us (88%)
  local copies, waits for them, and re-layouts  2.84 us (11%)
    pallas_call x1, Pallas kernels, local(): pl.pallas_call(functools.partial(kernel, pairs, cds), out_shape=jax.Shape...  22.2 us
    unnamed x2, local copies, waits for them, and re-layouts  2.84 us

profile of v1, /device:TPU:0, one launch (start us, length us, event | category | flops | bytes accessed | tf_op | source)
XLA Modules:
  0.0 25.0 jit_solution(17252111105669743328)
XLA Ops:
  0.0 1.4 %copy.4.flags = s32[32,2]{1,0:T(8,128)} copy(s32[32,2]{0,1:T(2,128)} %param.5) | data formatting | bytes 512 | tf_op args[2]
  1.4 22.2 %shard_map.37 = f32[64,256]{1,0:T(8,128)} custom-call(s32[32,2]{1,0:T(8,128)} %copy.4.flags, f32[128,256]{1,0:T(8,128)} %v_hbm.1, f32[256,1024]{1,0:T(8,128)} %a_hbm.1), custom_call_target="tpu_custom_call" | custom-call | tf_op jit(solution)/shard_map/pallas_call | solution.py:198
  23.6 1.5 %copy.6 = f32[64,256]{1,0:T(8,128)} copy(f32[64,256]{1,0:T(8,128)} %shard_map.37) | data formatting | bytes 131072

commit v2 on v1

--- a/solution.py
+++ b/solution.py
@@ -30,11 +30,12 @@
 
 
 def dot3(a_hi, a_lo, b_hi, b_lo):
-    d = functools.partial(jnp.dot, preferred_element_type=jnp.float32)
+    d = functools.partial(
+        lax.dot_general, dimension_numbers=(((1,), (1,)), ((), ())), preferred_element_type=jnp.float32)
     return d(a_hi, b_hi) + (d(a_lo, b_hi) + d(a_hi, b_lo))
 
 
-def kernel(pairs, cds, flags, v_hbm, a_hbm, out_ref, v, a, tiles, a_hi, a_lo, acc, land,
+def kernel(pairs, cds, flags_hbm, v_hbm, a_hbm, out_ref, flags, v, a, tiles, a_hi, a_lo, acc, land,
            load_sem, ssem, rsem, psend, precv, rs_send, rs_recv):
     nz = pairs // CORES
     me = lax.axis_index("pair")
@@ -48,6 +49,8 @@
 
     load_v = pltpu.make_async_copy(v_hbm, v, load_sem.at[0])
     load_v.start()
+    load_f = pltpu.make_async_copy(flags_hbm, flags, load_sem.at[2])
+    load_f.start()
     load_a = pltpu.make_async_copy(a_hbm, a, load_sem.at[1])
     load_a.start()
 
@@ -59,16 +62,17 @@
         @pl.when(has_next[d])
         def _():
             pl.semaphore_signal(barrier, inc=1, device_id={"pair": neighbour[d]}, device_id_type=MESH)
-    pl.semaphore_signal(barrier, inc=1, device_id={"pair": partner}, device_id_type=MESH)
     for j in range(1, cds):
         pl.semaphore_signal(barrier, inc=1, device_id={"cd": flip(cd, j)}, device_id_type=MESH)
-
+    pl.semaphore_signal(barrier, inc=1, device_id={"pair": partner}, device_id_type=MESH)
+
+    load_f.wait()
     load_v.wait()
     row_block = cd * pairs + me
-    own = v[:, :TILE] * flags[row_block, 0].astype(jnp.float32)
+    own = v[:, :TILE] * flags[0, row_block].astype(jnp.float32)
     for m in range(1, blocks):
-        own = own + v[:, m * TILE:(m + 1) * TILE] * flags[row_block, m].astype(jnp.float32)
-    tiles[me] = own
+        own = own + v[:, m * TILE:(m + 1) * TILE] * flags[m, row_block].astype(jnp.float32)
+    tiles[me] = own.T
 
     greeted = cds + jnp.minimum(z, 1) + jnp.minimum(nz - 1 - z, 1)
     pl.semaphore_wait(barrier, greeted)
@@ -94,7 +98,7 @@
         return z - s >= 0 if d == 0 else z + s < nz
 
     for c in range(CHUNKS):
-        for d in range(2):
+        for d in (1, 0):
             @pl.when(has_next[d])
             def _():
                 stream(d, 0, c, me).start()
@@ -106,24 +110,32 @@
     a_hi[...] = hi
     a_lo[...] = lo
 
-    def compute(d, s):
+    def compute(d, s, c):
         chip = origin(d, s)
-        for c in range(CHUNKS):
-            exchange(d, s, c, chip * CORES + 1 - core).wait_recv()
+        exchange(d, s, c, chip * CORES + 1 - core).wait_recv()
         halves = []
         for i in range(CORES):
             k = chip * CORES + i
-            t = tiles[k]
+            t = tiles[k, c * part:(c + 1) * part]
             g = cd * pairs + k
             halves.append(jnp.concatenate(
-                [t * flags[g, m].astype(jnp.float32) for m in range(blocks)], axis=1))
-        b_hi, b_lo = split(jnp.concatenate(halves, axis=0))
+                [t * flags[m, g].astype(jnp.float32) for m in range(blocks)], axis=0))
+        b_hi, b_lo = split(jnp.concatenate(halves, axis=1))
         cols = pl.ds(pl.multiple_of(chip * (CORES * TILE), CORES * TILE), CORES * TILE)
         prod = dot3(a_hi[:, cols], a_lo[:, cols], b_hi, b_lo)
         if s == 0:
-            acc[...] = prod
+            acc[c] = prod
         else:
-            acc[...] += prod
+            acc[c] += prod
+
+    def compute_step(s, c):
+        if s == 0:
+            compute(0, 0, c)
+        else:
+            for d in range(2):
+                @pl.when(valid(d, s))
+                def _():
+                    compute(d, s, c)
 
     for s in range(1, nz):
         for c in range(CHUNKS):
@@ -137,27 +149,19 @@
                         def _():
                             stream(d, s, c, k).start()
                     exchange(d, s, c, k).start()
-        if s == 1:
-            compute(0, 0)
-        else:
-            for d in range(2):
-                @pl.when(valid(d, s - 1))
-                def _():
-                    compute(d, s - 1)
-    for d in range(2):
-        @pl.when(valid(d, nz - 1))
-        def _():
-            compute(d, nz - 1)
-
-    def scatter(j):
+            compute_step(s - 1, c)
+
+    def scatter(j, c):
         q = flip(cd, j)
         return pltpu.make_async_remote_copy(
-            src_ref=acc.at[pl.ds(pl.multiple_of(q * rows, rows), rows)], dst_ref=land.at[j - 1],
-            send_sem=rs_send.at[j - 1], recv_sem=rs_recv.at[j - 1],
+            src_ref=acc.at[c, pl.ds(pl.multiple_of(q * rows, rows), rows)], dst_ref=land.at[j - 1, c],
+            send_sem=rs_send.at[j - 1, c], recv_sem=rs_recv.at[j - 1, c],
             device_id={"cd": q}, device_id_type=MESH)
 
-    for j in range(cds - 1, 0, -1):
-        scatter(j).start()
+    for c in range(CHUNKS):
+        compute_step(nz - 1, c)
+        for j in range(cds - 1, 0, -1):
+            scatter(j, c).start()
 
     for c in range(CHUNKS):
         exchange(0, 0, c, me).wait_send()
@@ -178,13 +182,19 @@
                         for c in range(CHUNKS):
                             stream(d, s, c, k).wait_send()
 
-    total = acc[pl.ds(pl.multiple_of(cd * rows, rows), rows)]
-    for j in range(1, cds):
-        scatter(j).wait_recv()
-        total = total + land[j - 1]
-    out_ref[...] = total
-    for j in range(1, cds):
-        scatter(j).wait_send()
+    totals = []
+    for c in range(CHUNKS):
+        total = acc[c, pl.ds(pl.multiple_of(cd * rows, rows), rows)]
+        for j in range(1, cds):
+            scatter(j, c).wait_recv()
+            total = total + land[j - 1, c]
+        totals.append(total)
+    for m in range(blocks):
+        out_ref[:, m * TILE:(m + 1) * TILE] = jnp.concatenate(
+            [t[:, m * part:(m + 1) * part] for t in totals], axis=1)
+    for c in range(CHUNKS):
+        for j in range(1, cds):
+            scatter(j, c).wait_send()
 
 
 def solution(mesh):
@@ -197,31 +207,32 @@
         rows = n // cds
         return pl.pallas_call(
             functools.partial(kernel, pairs, cds),
-            out_shape=jax.ShapeDtypeStruct((rows, ab), jnp.float32),
+            out_shape=pltpu.VMEM((rows, ab), jnp.float32),
             in_specs=[
-                pl.BlockSpec(memory_space=pltpu.SMEM),
+                pl.BlockSpec(memory_space=pl.ANY),
                 pl.BlockSpec(memory_space=pl.ANY),
                 pl.BlockSpec(memory_space=pl.ANY),
             ],
             out_specs=pl.BlockSpec(memory_space=pltpu.VMEM),
             scratch_shapes=[
+                pltpu.SMEM(keep_tiles.shape[::-1], jnp.int32),
                 pltpu.VMEM(integrals.shape, jnp.float32),
                 pltpu.VMEM((n, depth), jnp.float32),
                 pltpu.VMEM((pairs, TILE, TILE), jnp.float32),
                 pltpu.VMEM((n, depth), jnp.bfloat16),
                 pltpu.VMEM((n, depth), jnp.bfloat16),
-                pltpu.VMEM((n, ab), jnp.float32),
-                pltpu.VMEM((cds - 1, rows, ab), jnp.float32),
-                pltpu.SemaphoreType.DMA((2,)),
-                pltpu.SemaphoreType.DMA((2, nz, CHUNKS)),
-                pltpu.SemaphoreType.DMA((2, nz, CHUNKS)),
-                pltpu.SemaphoreType.DMA((2, nz, CHUNKS)),
-                pltpu.SemaphoreType.DMA((2, nz, CHUNKS)),
-                pltpu.SemaphoreType.DMA((cds - 1,)),
-                pltpu.SemaphoreType.DMA((cds - 1,)),
+                pltpu.VMEM((CHUNKS, n, ab // CHUNKS), jnp.float32),
+                pltpu.VMEM((cds - 1, CHUNKS, rows, ab // CHUNKS), jnp.float32),
+                pltpu.SemaphoreType.DMA((3,)),
+                pltpu.SemaphoreType.DMA((2, nz, CHUNKS)),
+                pltpu.SemaphoreType.DMA((2, nz, CHUNKS)),
+                pltpu.SemaphoreType.DMA((2, nz, CHUNKS)),
+                pltpu.SemaphoreType.DMA((2, nz, CHUNKS)),
+                pltpu.SemaphoreType.DMA((cds - 1, CHUNKS)),
+                pltpu.SemaphoreType.DMA((cds - 1, CHUNKS)),
             ],
             compiler_params=pltpu.CompilerParams(collective_id=0, has_side_effects=True),
-        )(keep_tiles, integrals, amplitudes)
+        )(keep_tiles.T, integrals, amplitudes)
 
     placed = (P("pair", "cd"), P(("cd", "pair"), None), P())
     return jax.shard_map(

time: 25.3 us -> 21.7 us (0.86)
  local copies, waits for them, and re-layouts: 2.84 us -> 0.63 us
  Pallas kernels: 22.2 us -> 20.9 us
    unnamed x2 -> x1, local copies, waits for them, and re-layouts: 2.84 us -> 0.63 us
    pallas_call x1, Pallas kernels: 22.2 us -> 20.9 us  [local(): pl.pallas_call(functools.partial(kernel, pairs, cds), out_shape=pltpu.VME...]
where the time goes in v2:
time: 21.7 us; the launch traced here: 21.6 us
  Pallas kernels  20.9 us (96%)
  local copies, waits for them, and re-layouts  0.63 us (3%)
    pallas_call x1, Pallas kernels, local(): pl.pallas_call(functools.partial(kernel, pairs, cds), out_shape=pltpu.VME...  20.9 us
    unnamed x1, local copies, waits for them, and re-layouts  0.63 us

profile of v2, /device:TPU:0, one launch (start us, length us, event | category | flops | bytes accessed | tf_op | source)
XLA Modules:
  0.0 21.6 jit_solution(8267819927724920061)
XLA Ops:
  0.0 20.9 %shard_map.37 = f32[64,256]{1,0:T(8,128)S(1)} custom-call(s32[2,32]{1,0:T(2,128)} %bitcast.1, f32[128,256]{1,0:T(8,128)} %v_hbm.1, f32[256,1024]{1,0:T(8,128)} %a_hbm.1), custom_call_target="tpu_custom_call" | custom-call | tf_op jit(solution)/shard_map/pallas_call | solution.py:208
  20.9 0.6 %copy.5 = f32[64,256]{1,0:T(8,128)} copy(f32[64,256]{1,0:T(8,128)S(1)} %shard_map.37) | data formatting | bytes 131072

commit v3 on v2

--- a/solution.py
+++ b/solution.py
@@ -47,6 +47,9 @@
     part = TILE // CHUNKS
     rows = out_ref.shape[0]
 
+    def valid(d, s):
+        return z - s >= 0 if d == 0 else z + s < nz
+
     load_v = pltpu.make_async_copy(v_hbm, v, load_sem.at[0])
     load_v.start()
     load_f = pltpu.make_async_copy(flags_hbm, flags, load_sem.at[2])
@@ -59,9 +62,11 @@
 
     barrier = pltpu.get_barrier_semaphore()
     for d in range(2):
-        @pl.when(has_next[d])
-        def _():
-            pl.semaphore_signal(barrier, inc=1, device_id={"pair": neighbour[d]}, device_id_type=MESH)
+        for s in range(nz - 1):
+            far = me + (s + 1) * CORES if d == 0 else me - (s + 1) * CORES
+            @pl.when(valid(1 - d, s + 1))
+            def _():
+                pl.semaphore_signal(barrier, inc=1, device_id={"pair": far}, device_id_type=MESH)
     for j in range(1, cds):
         pl.semaphore_signal(barrier, inc=1, device_id={"cd": flip(cd, j)}, device_id_type=MESH)
     pl.semaphore_signal(barrier, inc=1, device_id={"pair": partner}, device_id_type=MESH)
@@ -74,15 +79,16 @@
         own = own + v[:, m * TILE:(m + 1) * TILE] * flags[m, row_block].astype(jnp.float32)
     tiles[me] = own.T
 
-    greeted = cds + jnp.minimum(z, 1) + jnp.minimum(nz - 1 - z, 1)
+    greeted = cds + nz - 1
     pl.semaphore_wait(barrier, greeted)
 
     def stream(d, s, c, k):
         r = pl.ds(c * part, part)
+        far = me + (s + 1) * CORES if d == 0 else me - (s + 1) * CORES
         return pltpu.make_async_remote_copy(
             src_ref=tiles.at[k, r], dst_ref=tiles.at[k, r],
             send_sem=ssem.at[d, s, c], recv_sem=rsem.at[d, s, c],
-            device_id={"pair": neighbour[d]}, device_id_type=MESH)
+            device_id={"pair": far}, device_id_type=MESH)
 
     def exchange(d, s, c, k):
         r = pl.ds(c * part, part)
@@ -94,14 +100,12 @@
     def origin(d, s):
         return z - s if d == 0 else z + s
 
-    def valid(d, s):
-        return z - s >= 0 if d == 0 else z + s < nz
-
-    for c in range(CHUNKS):
-        for d in (1, 0):
-            @pl.when(has_next[d])
-            def _():
-                stream(d, 0, c, me).start()
+    for c in range(CHUNKS):
+        for s in range(nz - 2, -1, -1):
+            for d in (1, 0):
+                @pl.when(valid(1 - d, s + 1))
+                def _():
+                    stream(d, s, c, me).start()
     for c in range(CHUNKS):
         exchange(0, 0, c, me).start()
 
@@ -144,10 +148,6 @@
                 def _():
                     k = origin(d, s) * CORES + core
                     stream(d, s - 1, c, k).wait_recv()
-                    if s < nz - 1:
-                        @pl.when(has_next[d])
-                        def _():
-                            stream(d, s, c, k).start()
                     exchange(d, s, c, k).start()
             compute_step(s - 1, c)
 
@@ -166,9 +166,10 @@
     for c in range(CHUNKS):
         exchange(0, 0, c, me).wait_send()
         for d in range(2):
-            @pl.when(has_next[d])
-            def _():
-                stream(d, 0, c, me).wait_send()
+            for s in range(nz - 1):
+                @pl.when(valid(1 - d, s + 1))
+                def _():
+                    stream(d, s, c, me).wait_send()
     for s in range(1, nz):
         for d in range(2):
             @pl.when(valid(d, s))
@@ -176,11 +177,6 @@
                 k = origin(d, s) * CORES + core
                 for c in range(CHUNKS):
                     exchange(d, s, c, k).wait_send()
-                if s < nz - 1:
-                    @pl.when(has_next[d])
-                    def _():
-                        for c in range(CHUNKS):
-                            stream(d, s, c, k).wait_send()
 
     totals = []
     for c in range(CHUNKS):

time: 21.7 us -> 20.1 us (0.926)
  Pallas kernels: 20.9 us -> 19.3 us
    pallas_call x1, Pallas kernels: 20.9 us -> 19.3 us  [local(): pl.pallas_call(functools.partial(kernel, pairs, cds), out_shape=pltpu.VME...]
where the time goes in v3:
time: 20.1 us; the launch traced here: 20 us
  Pallas kernels  19.3 us (96%)
  local copies, waits for them, and re-layouts  0.63 us (3%)
    pallas_call x1, Pallas kernels, local(): pl.pallas_call(functools.partial(kernel, pairs, cds), out_shape=pltpu.VME...  19.3 us
    unnamed x1, local copies, waits for them, and re-layouts  0.63 us

profile of v3, /device:TPU:0, one launch (start us, length us, event | category | flops | bytes accessed | tf_op | source)
XLA Modules:
  0.0 20.0 jit_solution(14910519393502186407)
XLA Ops:
  0.0 19.3 %shard_map.37 = f32[64,256]{1,0:T(8,128)S(1)} custom-call(s32[2,32]{1,0:T(2,128)} %bitcast.1, f32[128,256]{1,0:T(8,128)} %v_hbm.1, f32[256,1024]{1,0:T(8,128)} %a_hbm.1), custom_call_target="tpu_custom_call" | custom-call | tf_op jit(solution)/shard_map/pallas_call | solution.py:204
  19.4 0.6 %copy.5 = f32[64,256]{1,0:T(8,128)} copy(f32[64,256]{1,0:T(8,128)S(1)} %shard_map.37) | data formatting | bytes 131072

commit v4 on v3

--- a/solution.py
+++ b/solution.py
@@ -9,7 +9,7 @@
 
 TILE = 128
 CORES = 2
-CHUNKS = 2
+CHUNKS = 1
 MESH = pl.DeviceIdType.MESH
 
 
@@ -100,8 +100,8 @@
     def origin(d, s):
         return z - s if d == 0 else z + s
 
-    for c in range(CHUNKS):
-        for s in range(nz - 2, -1, -1):
+    for s in range(nz - 2, -1, -1):
+        for c in range(CHUNKS):
             for d in (1, 0):
                 @pl.when(valid(1 - d, s + 1))
                 def _():

time: 20.1 us -> 19.2 us (0.955)
  Pallas kernels: 19.3 us -> 18.4 us
    pallas_call x1, Pallas kernels: 19.3 us -> 18.4 us  [local(): pl.pallas_call(functools.partial(kernel, pairs, cds), out_shape=pltpu.VME...]
where the time goes in v4:
time: 19.2 us; the launch traced here: 19.1 us
  Pallas kernels  18.4 us (96%)
  local copies, waits for them, and re-layouts  0.63 us (3%)
    pallas_call x1, Pallas kernels, local(): pl.pallas_call(functools.partial(kernel, pairs, cds), out_shape=pltpu.VME...  18.4 us
    unnamed x1, local copies, waits for them, and re-layouts  0.63 us

profile of v4, /device:TPU:0, one launch (start us, length us, event | category | flops | bytes accessed | tf_op | source)
XLA Modules:
  0.0 19.1 jit_solution(11863778521104568246)
XLA Ops:
  0.0 18.4 %shard_map.37 = f32[64,256]{1,0:T(8,128)S(1)} custom-call(s32[2,32]{1,0:T(2,128)} %bitcast.1, f32[128,256]{1,0:T(8,128)} %v_hbm.1, f32[256,1024]{1,0:T(8,128)} %a_hbm.1), custom_call_target="tpu_custom_call" | custom-call | tf_op jit(solution)/shard_map/pallas_call | solution.py:204
  18.4 0.6 %copy.5 = f32[64,256]{1,0:T(8,128)} copy(f32[64,256]{1,0:T(8,128)S(1)} %shard_map.37) | data formatting | bytes 131072
